TPU v7x, 256 devices: a whole 4x4x8 slice. The times are simulated.
256 devices in a mesh: ctx: 32 (over y, x, core), head: 8 (over z).
Axes of the slice: x: 4, y: 4, z: 8, core: 2. Of those that a mesh axis runs over, the one named last changes fastest.
Arguments:
- query_rows: bfloat16 [32768, 4096], P('ctx', 'head'), may hold values from -6 to 6
- key_rows: bfloat16 [32768, 4096], P('ctx', 'head'), may hold values from -6 to 6
- value_rows: bfloat16 [32768, 4096], P('ctx', 'head'), may hold values from -6 to 6
- frequencies: bfloat16 [32, 128, 128], P('head'), may hold values from -4.1875 to 4.1875
- norm_gain: bfloat16 [4096], P('head'), may hold values from 0.25 to 1.75
- out_weight: bfloat16 [4096, 4096], P(None, 'head'), may hold values from -0.09375 to 0.09375
Outputs:
- projected: bfloat16 [32768, 4096], P('ctx', 'head')
All inputs are finite; a program needn't handle non-finite values.
Results may differ from a plain program's by a relative error of at most 0.009.
Values may be sent and summed in bfloat16 or wider, within the bound.
A program may use at most 128 MiB of HBM per device.

v0:
```python
import math
import jax
import jax.numpy as jnp
from jax import lax
from jax.sharding import PartitionSpec as P


def carried_in(value, axis, join, neutral):
    count, mine = (lax.axis_size(axis), lax.axis_index(axis))
    pieces = lax.all_gather(value, axis)
    subtotal = jnp.full_like(value, 0) + jnp.asarray(neutral, value.dtype)

    def turn(position, subtotal):
        longer = join(subtotal, pieces[position])
        return jnp.where(position < mine, longer, subtotal)

    return lax.fori_loop(0, count - 1, turn, subtotal)


def features_of(inputs, frequencies, freq_count):
    phases = jnp.einsum("bthd,hdf->bthf", inputs, frequencies, preferred_element_type=jnp.float32)
    joined = jnp.concatenate([jnp.cos(phases), jnp.sin(phases)], axis=-1)
    return (joined * (1.0 / math.sqrt(freq_count))).astype(jnp.bfloat16)


def add_states(first_part, second_part):
    return first_part + second_part


def local(query_rows, key_rows, value_rows, frequencies, norm_gain, out_weight):
    row_count = query_rows.shape[0]
    heads_here, head_width, freq_count = frequencies.shape
    span_rows = min(512, row_count)
    span_count = row_count // span_rows
    span_shape = (span_count, span_rows, heads_here, head_width)
    query_spans = query_rows.reshape(span_shape)
    key_spans = key_rows.reshape(span_shape)
    value_spans = value_rows.reshape(span_shape)
    query_feat = features_of(query_spans, frequencies, freq_count)
    key_feat = features_of(key_spans, frequencies, freq_count)
    span_states = jnp.einsum(
        "bthf,bthd->bhfd", key_feat, value_spans, preferred_element_type=jnp.float32
    )
    shard_total = jnp.sum(span_states, axis=0)
    preceding = carried_in(shard_total, "ctx", add_states, jnp.zeros_like(shard_total))
    running_sums = jnp.cumsum(span_states, axis=0)
    earlier_local = jnp.concatenate([jnp.zeros_like(span_states[:1]), running_sums[:-1]], axis=0)
    carried_low = (preceding[None] + earlier_local).astype(jnp.bfloat16)
    causal = jnp.arange(span_rows)[:, None] >= jnp.arange(span_rows)[None, :]
    scores = jnp.einsum("bthf,bshf->bhts", query_feat, key_feat, preferred_element_type=jnp.float32)
    scores = jnp.where(causal[None, None], scores, jnp.zeros_like(scores)).astype(jnp.bfloat16)
    local_part = jnp.einsum(
        "bhts,bshd->bthd", scores, value_spans, preferred_element_type=jnp.float32
    )
    prior_part = jnp.einsum(
        "bthf,bhfd->bthd", query_feat, carried_low, preferred_element_type=jnp.float32
    )
    attended = local_part + prior_part
    gain_table = norm_gain.astype(jnp.float32).reshape(heads_here, head_width)
    mean_square = jnp.mean(attended * attended, axis=-1, keepdims=True)
    normed = (attended * lax.rsqrt(mean_square + 1e-06) * gain_table[None, None]).astype(
        jnp.bfloat16
    )
    normed = normed.reshape(row_count, heads_here * head_width)
    projected = jnp.dot(
        lax.all_gather(normed, "head", axis=1, tiled=True),
        out_weight,
        preferred_element_type=jnp.float32,
    )
    return projected.astype(jnp.bfloat16)


def solution(mesh):
    return jax.shard_map(
        local,
        mesh=mesh,
        in_specs=(
            P("ctx", "head"),
            P("ctx", "head"),
            P("ctx", "head"),
            P("head", None, None),
            P("head"),
            P(None, "head"),
        ),
        out_specs=P("ctx", "head"),
        check_vma=False,
    )
```

profile of v0, /device:TPU:1, one launch (start us, length us, event | category | flops | bytes accessed | tf_op | source)
XLA Modules:
  0.0 270.1 jit_solution(10711758108041598171)
XLA Ops:
  6.5 1.4 reshape.34
  8.4 9.7 %cosine_bitcast_fusion.1 = (f32[2,512,4,128]{1,3,0,2:T(8,128)}, f32[2,512,4,128]{1,3,0,2:T(8,128)}) fusion(bf16[2,512,4,128]{3,2,1,0:T(4,128)(2,1)S(1)} %reshape.34, bf16[4,128,128]{2,1,0:T(8,128)(2,1)S(1)} %copy-done), kind=kOutput, calls=%fused_computation.16 | convolution fusion | flops 134217728 | bytes 5373952 | tf_op jit(solution)/shard_map/bthd,hdf->bthf/dot_general | solution.py:21
  18.1 9.7 %cosine_bitcast_fusion = (f32[2,512,4,128]{1,3,0,2:T(8,128)}, f32[2,512,4,128]{1,3,0,2:T(8,128)}) fusion(bf16[2,512,4,128]{3,2,1,0:T(4,128)(2,1)S(1)} %reshape.35, bf16[4,128,128]{2,1,0:T(8,128)(2,1)S(1)} %copy-done), kind=kOutput, calls=%fused_computation.14 | convolution fusion | flops 134217728 | bytes 5373952 | tf_op jit(solution)/shard_map/bthd,hdf->bthf/dot_general | solution.py:21
  28.2 4.4 %fusion.1 = (bf16[2,512,4,256]{1,3,0,2:T(8,128)(2,1)S(1)}, bf16[2,512,4,256]{1,3,0,2:T(8,128)(2,1)S(1)}) fusion(f32[2,512,4,128]{1,3,0,2:T(8,128)} %get-tuple-element.109, f32[2,512,4,128]{1,3,0,2:T(8,128)} %get-tuple-element.108, f32[2,512,4,128]{1,3,0,2:T(8,128)} %get-tuple-element.111, f32[2,512,4,128]{1,3,0,2:T(8,128)} %get-tuple-element.110), kind=kLoop, calls=%fused_computation.4 | loop fusion | flops 6291456 | bytes 12582912 | tf_op jit(solution)/shard_map/convert_element_type | solution.py:23
  32.6 2.5 fusion.28
  35.2 1.3 fusion.37
  36.7 5.8 %fusion = f32[2,4,512,128]{2,3,1,0:T(8,128)} fusion(pred[512,512]{1,0:T(8,128)(4,1)S(1)} %iota_compare_fusion, bf16[2,512,4,256]{1,3,0,2:T(8,128)(2,1)} %copy-done.1, bf16[2,512,4,256]{1,3,0,2:T(8,128)(2,1)S(1)} %get-tuple-element.116, bf16[2,512,4,128]{3,2,1,0:T(4,128)(2,1)} %copy-done.4), kind=kOutput, calls=%fused_computation.2 | convolution fusion | flops 1614807040 | bytes 7602176 | tf_op jit(solution)/shard_map/bhts,bshd->bthd/dot_general | solution.py:52
  42.5 74.5 %all-gather.6.cloned.1.call-done = f32[128,256,128]{2,1,0:T(8,128)} async-done(((f32[4,256,128]{2,1,0:T(8,128)}), f32[128,256,128]{2,1,0:T(8,128)}) %all-gather.6.cloned.1.call-update) | async-done | bytes 16777232 | tf_op jit(solution)/shard_map/all_gather | solution.py:10
  117.0 38.4 %while.14 = (s32[]{:T(128)}, f32[4,256,128]{2,1,0:T(8,128)S(1)}, s32[]{:T(128)}, f32[32,4,256,128]{3,2,1,0:T(8,128)}, s32[]{:T(128)}, /*index=5*/s32[]{:T(128)}) while((s32[]{:T(128)}, f32[4,256,128]{2,1,0:T(8,128)S(1)}, s32[]{:T(128)}, f32[32,4,256,128]{3,2,1,0:T(8,128)}, s32[]{:T(128)}, /*index=5*/s32[]{:T(128)}) %tuple.44), condition=%wide.region_2.3_spmd.clone, body=%wide.region_1.2_spmd.clone.sunk | while | flops 393220 | bytes 1572957 | solution.py:17
  118.3 1.2 add_select_fusion.2
  119.5 1.2 add_select_fusion.2
  120.7 1.2 add_select_fusion.2
  122.0 1.2 add_select_fusion.2
  123.2 1.2 add_select_fusion.2
  124.5 1.2 add_select_fusion.2
  125.7 1.2 add_select_fusion.2
  126.9 1.2 add_select_fusion.2
  128.2 1.2 add_select_fusion.2
  129.4 1.2 add_select_fusion.2
  130.7 1.2 add_select_fusion.2
  131.9 1.2 add_select_fusion.2
  133.1 1.2 add_select_fusion.2
  134.4 1.2 add_select_fusion.2
  135.6 1.2 add_select_fusion.2
  136.9 1.2 add_select_fusion.2
  138.1 1.2 add_select_fusion.2
  139.3 1.2 add_select_fusion.2
  140.6 1.2 add_select_fusion.2
  141.8 1.2 add_select_fusion.2
  155.5 2.2 multiply_reduce_fusion
  159.8 93.4 %all-gather.4.cloned.1.call-done = bf16[1024,4096]{1,0:T(8,128)(2,1)} async-done(((bf16[1024,512]{1,0:T(8,128)(2,1)}), bf16[1024,4096]{1,0:T(8,128)(2,1)}) %all-gather.4.cloned.1.call-update) | async-done | bytes 8388624 | tf_op jit(solution)/shard_map/all_gather | solution.py:66
  253.2 10.0 %convolution_convert_fusion = bf16[1024,512]{1,0:T(8,128)(2,1)} fusion(bf16[1024,4096]{1,0:T(8,128)(2,1)} %all-gather.4.cloned.1.call-done, bf16[4096,512]{1,0:T(8,128)(2,1)} %param.13), kind=kOutput, calls=%fused_computation.23 | convolution fusion | flops 4295491584 | bytes 13631488 | tf_op jit(solution)/shard_map/dot_general | solution.py:65
  (37 shorter events, 16.5 us)
Async XLA Ops:
  6.5 1.9 copy-start
  6.5 1.6 copy-start.2
  6.5 110.5 %all-gather.6.cloned.1.call-start = ((), (), s32[]{:S(2)}) async-start(), calls=%async_computation.1 | async-start | bytes 17301504 | tf_op jit(solution)/shard_map/all_gather | solution.py:10
  18.1 9.8 %copy-start.3 = (bf16[1024,512]{1,0:T(8,128)(2,1)S(1)}, bf16[1024,512]{1,0:T(8,128)(2,1)}, u32[]{:S(2)}) copy-start(bf16[1024,512]{1,0:T(8,128)(2,1)} %param.10) | copy-start | bytes 3145732
  28.2 4.4 %copy-start.4 = (bf16[2,512,4,128]{3,2,1,0:T(4,128)(2,1)}, bf16[2,512,4,128]{3,2,1,0:T(4,128)(2,1)S(1)}, u32[]{:S(2)}) copy-start(bf16[2,512,4,128]{3,2,1,0:T(4,128)(2,1)S(1)} %reshape.36) | copy-start | bytes 3145732
  32.6 2.5 copy-start.1
  35.1 1.5 copy-start.5
  35.2 218.1 %all-gather.4.cloned.1.call-start = ((), (), s32[]{:S(2)}) async-start(), calls=%async_computation | async-start | bytes 9437184 | tf_op jit(solution)/shard_map/all_gather | solution.py:66
Sparse Core Ops, SparseCore 0:
  35.3 81.7 all-gather.5
  160.0 93.2 all-gather.3
where the time goes:
time: 272 us; the launch traced here: 270 us
  waiting for transfers between devices  168 us (62%)
  other arithmetic  43.8 us (16%)
  matrix products  40 us (15%)
  between operations  13.6 us (5%)
  local copies, waits for them, and re-layouts  4.07 us (1%)
    all_gather x1, waiting for transfers between devices, local(): lax.all_gather(normed, 'head', axis=1, tiled=True)  93.4 us
    all_gather x1, waiting for transfers between devices, carried_in(): pieces = lax.all_gather(value, axis)  74.5 us
    select_n x31, other arithmetic, turn(): return jnp.where(position < mine, longer, subtotal)  37.7 us
    dot_general x2, matrix products, features_of(): jnp.einsum('bthd,hdf->bthf', inputs, frequencies, preferred_element_type=...  19.5 us
    dot_general x1, matrix products, local(): jnp.dot(lax.all_gather(normed, 'head', axis=1, tiled=True), out_weight, p...  10 us
    dot_general x1, matrix products, local(): jnp.einsum('bhts,bshd->bthd', scores, value_spans, preferred_element_type...  5.83 us
  transfers between devices with their start and end apart: 2, of which 2 were waited for; matrix products, arithmetic and copies ran while one was open for 3% of the time, Pallas kernels for 0%

commit v1 on v0

--- a/solution.py
+++ b/solution.py
@@ -3,6 +3,7 @@
 import jax.numpy as jnp
 from jax import lax
 from jax.sharding import PartitionSpec as P
+from jax.lax import all_to_all, axis_size
 
 
 def carried_in(value, axis, join, neutral):
@@ -62,11 +63,16 @@
         jnp.bfloat16
     )
     normed = normed.reshape(row_count, heads_here * head_width)
-    projected = jnp.dot(
-        lax.all_gather(normed, "head", axis=1, tiled=True),
-        out_weight,
-        preferred_element_type=jnp.float32,
-    )
+
+    def read_face(u, peer_axis):
+        return jnp.concatenate(
+            all_to_all(
+                jnp.stack([u for _ in range(axis_size(peer_axis))], axis=0), peer_axis, 0, 0
+            ),
+            1,
+        )
+
+    projected = jnp.dot(read_face(normed, "head"), out_weight, preferred_element_type=jnp.float32)
     return projected.astype(jnp.bfloat16)
 
 

time: 272 us -> 369 us (1.36)
  blocking collectives: 0 us -> 193 us
  waiting for transfers between devices: 168 us -> 74.6 us
  matrix products: 40 us -> 35.4 us
    all_to_all x0 -> x1, blocking collectives: none -> 193 us  [read_face(): all_to_all(jnp.stack([u for _ in range(axis_size(peer_axis))], axis=0), p...]
    all_gather x1 -> x0, waiting for transfers between devices: 93.4 us -> none  [local(): lax.all_gather(normed, 'head', axis=1, tiled=True)]
    dot_general x1, matrix products: 10 us -> 5.49 us  [local(): jnp.dot(read_face(normed, 'head'), out_weight, preferred_element_type=jnp...]
  transfers between devices with their start and end apart: 2 -> 1, of which waited for: 2 -> 1; matrix products, arithmetic and copies ran while one was open for 3% -> 2% of each run, Pallas kernels for 0% -> 0%
where the time goes in v1:
time: 369 us; the launch traced here: 367 us
  blocking collectives  193 us (52%)
  waiting for transfers between devices  74.6 us (20%)
  other arithmetic  43.5 us (12%)
  matrix products  35.4 us (10%)
  between operations  13.6 us (4%)
  local copies, waits for them, and re-layouts  6.26 us (2%)
    all_to_all x1, blocking collectives, read_face(): all_to_all(jnp.stack([u for _ in range(axis_size(peer_axis))], axis=0), p...  193 us
    all_gather x1, waiting for transfers between devices, carried_in(): pieces = lax.all_gather(value, axis)  74.6 us
    select_n x31, other arithmetic, turn(): return jnp.where(position < mine, longer, subtotal)  37.7 us
    dot_general x2, matrix products, features_of(): jnp.einsum('bthd,hdf->bthf', inputs, frequencies, preferred_element_type=...  19.4 us
  transfers between devices with their start and end apart: 1, of which 1 were waited for; matrix products, arithmetic and copies ran while one was open for 2% of the time, Pallas kernels for 0%

profile of v1, /device:TPU:1, one launch (start us, length us, event | category | flops | bytes accessed | tf_op | source)
XLA Modules:
  0.0 366.9 jit_solution(18034599964499348434)
XLA Ops:
  6.5 1.4 reshape.39
  7.9 1.3 reshape.40
  9.3 9.7 %cosine_bitcast_fusion.1 = (f32[2,512,4,128]{1,3,0,2:T(8,128)}, f32[2,512,4,128]{1,3,0,2:T(8,128)}) fusion(bf16[2,512,4,128]{3,2,1,0:T(4,128)(2,1)S(1)} %reshape.39, bf16[4,128,128]{2,1,0:T(8,128)(2,1)S(1)} %copy-done), kind=kOutput, calls=%fused_computation.16 | convolution fusion | flops 134217728 | bytes 5373952 | tf_op jit(solution)/shard_map/bthd,hdf->bthf/dot_general | solution.py:22
  19.0 9.7 %cosine_bitcast_fusion = (f32[2,512,4,128]{1,3,0,2:T(8,128)}, f32[2,512,4,128]{1,3,0,2:T(8,128)}) fusion(bf16[2,512,4,128]{3,2,1,0:T(4,128)(2,1)S(1)} %reshape.40, bf16[4,128,128]{2,1,0:T(8,128)(2,1)S(1)} %copy-done), kind=kOutput, calls=%fused_computation.14 | convolution fusion | flops 134217728 | bytes 5373952 | tf_op jit(solution)/shard_map/bthd,hdf->bthf/dot_general | solution.py:22
  29.8 4.1 %fusion.1 = (bf16[2,512,4,256]{1,3,0,2:T(8,128)(2,1)S(1)}, bf16[2,512,4,256]{1,3,0,2:T(8,128)(2,1)S(1)}) fusion(f32[2,512,4,128]{1,3,0,2:T(8,128)} %get-tuple-element.109, f32[2,512,4,128]{1,3,0,2:T(8,128)} %get-tuple-element.108, f32[2,512,4,128]{1,3,0,2:T(8,128)} %get-tuple-element.111, f32[2,512,4,128]{1,3,0,2:T(8,128)} %get-tuple-element.110), kind=kLoop, calls=%fused_computation.4 | loop fusion | flops 6291456 | bytes 12582912 | tf_op jit(solution)/shard_map/convert_element_type | solution.py:24
  34.0 2.5 fusion.28
  36.5 1.3 fusion.37
  38.0 5.8 %fusion = f32[2,4,512,128]{2,3,1,0:T(8,128)} fusion(pred[512,512]{1,0:T(8,128)(4,1)S(1)} %iota_compare_fusion, bf16[2,512,4,256]{1,3,0,2:T(8,128)(2,1)} %copy-done.2, bf16[2,512,4,256]{1,3,0,2:T(8,128)(2,1)S(1)} %get-tuple-element.116, bf16[2,512,4,128]{3,2,1,0:T(4,128)(2,1)} %reshape.41), kind=kOutput, calls=%fused_computation.2 | convolution fusion | flops 1614807040 | bytes 7602176 | tf_op jit(solution)/shard_map/bhts,bshd->bthd/dot_general | solution.py:53
  43.8 74.6 %all-gather.3.cloned.1.call-done = f32[128,256,128]{2,1,0:T(8,128)} async-done(((f32[4,256,128]{2,1,0:T(8,128)}), f32[128,256,128]{2,1,0:T(8,128)}) %all-gather.3.cloned.1.call-update) | async-done | bytes 16777232 | tf_op jit(solution)/shard_map/all_gather | solution.py:11
  118.4 38.4 %while.14 = (s32[]{:T(128)}, f32[4,256,128]{2,1,0:T(8,128)S(1)}, s32[]{:T(128)}, f32[32,4,256,128]{3,2,1,0:T(8,128)}, s32[]{:T(128)}, /*index=5*/s32[]{:T(128)}) while((s32[]{:T(128)}, f32[4,256,128]{2,1,0:T(8,128)S(1)}, s32[]{:T(128)}, f32[32,4,256,128]{3,2,1,0:T(8,128)}, s32[]{:T(128)}, /*index=5*/s32[]{:T(128)}) %tuple.42), condition=%wide.region_2.3_spmd.clone, body=%wide.region_1.2_spmd.clone.sunk | while | flops 393220 | bytes 1572957 | solution.py:18
  119.6 1.2 add_select_fusion.2
  120.8 1.2 add_select_fusion.2
  122.1 1.2 add_select_fusion.2
  123.3 1.2 add_select_fusion.2
  124.6 1.2 add_select_fusion.2
  125.8 1.2 add_select_fusion.2
  127.0 1.2 add_select_fusion.2
  128.3 1.2 add_select_fusion.2
  129.5 1.2 add_select_fusion.2
  130.8 1.2 add_select_fusion.2
  132.0 1.2 add_select_fusion.2
  133.2 1.2 add_select_fusion.2
  134.5 1.2 add_select_fusion.2
  135.7 1.2 add_select_fusion.2
  137.0 1.2 add_select_fusion.2
  138.2 1.2 add_select_fusion.2
  139.4 1.2 add_select_fusion.2
  140.7 1.2 add_select_fusion.2
  141.9 1.2 add_select_fusion.2
  156.8 2.2 multiply_reduce_fusion
  161.7 192.9 %all_to_all.5 = bf16[8,1024,512]{1,2,0:T(8,128)(2,1)S(1)} all-to-all(bf16[8,1024,512]{1,2,0:T(8,128)(2,1)S(1)} %stack.3), channel_id=1, replica_groups=mesh['ctx'=32,'head'=8] {'head'}, dimensions={0} | all-to-all | bytes 16777216 | tf_op jit(solution)/shard_map/all_to_all | solution.py:69
  354.5 5.5 %convolution_convert_fusion = bf16[1024,512]{1,0:T(8,128)(2,1)} fusion(bf16[1024,4096]{0,1:T(8,128)(2,1)S(1)} %bitcast.43, bf16[4096,512]{1,0:T(8,128)(2,1)S(1)} %copy-done.6), kind=kOutput, calls=%fused_computation.23 | convolution fusion | flops 4295491584 | bytes 13631488 | tf_op jit(solution)/shard_map/dot_general | solution.py:75
  (38 shorter events, 18.5 us)
Async XLA Ops:
  6.5 2.7 copy-start
  6.5 111.8 %all-gather.3.cloned.1.call-start = ((), (), s32[]{:S(2)}) async-start(), calls=%async_computation.1 | async-start | bytes 17301504 | tf_op jit(solution)/shard_map/all_gather | solution.py:11
  19.0 9.7 %copy-start.3 = (bf16[1024,512]{1,0:T(8,128)(2,1)S(1)}, bf16[1024,512]{1,0:T(8,128)(2,1)}, u32[]{:S(2)}) copy-start(bf16[1024,512]{1,0:T(8,128)(2,1)} %param.10) | copy-start | bytes 3145732
  29.8 4.1 %copy-start.4 = (bf16[2,512,4,128]{3,2,1,0:T(4,128)(2,1)S(1)}, bf16[2,512,4,128]{3,2,1,0:T(4,128)(2,1)}, u32[]{:S(2)}) copy-start(bf16[2,512,4,128]{3,2,1,0:T(4,128)(2,1)} %reshape.41) | copy-start | bytes 3145732
  33.9 2.5 copy-start.2
  36.5 1.5 copy-start.5
  161.7 192.9 %copy-start.6 = (bf16[4096,512]{1,0:T(8,128)(2,1)S(1)}, bf16[4096,512]{1,0:T(8,128)(2,1)}, u32[]{:S(2)}) copy-start(bf16[4096,512]{1,0:T(8,128)(2,1)} %param.13) | copy-start | bytes 12582916
  354.5 5.5 %copy-start.1 = (bf16[4,128,128]{2,1,0:T(8,128)(2,1)S(1)}, bf16[4,128,128]{2,1,0:T(8,128)(2,1)}, u32[]{:S(2)}) copy-start(bf16[4,128,128]{2,1,0:T(8,128)(2,1)} %param.11) | copy-start | bytes 393220
Sparse Core Ops, SparseCore 0:
  36.6 81.7 all-gather.2
